TPU v7x, 256 devices: a whole 4x4x8 slice. The times are simulated.
256 devices in a mesh: row: 16 (over z, core), col: 16 (over y, x).
Axes of the slice: x: 4, y: 4, z: 8, core: 2. Of those that a mesh axis runs over, the one named last changes fastest.
Arguments:
- start_basis: float32 [32, 131072], P(None, ('row', 'col')), may hold values from -6 to 6
- degrees: float32 [131072], P(('row', 'col')), may hold values from 0.5 to 1.5
- tiles: float32 [8192, 256, 256], P(('row', 'col')), may hold values from -0.046875 to 0.046875
- tile_rows: int32 [16, 512], P('row', 'col'), may hold values from 0 to 31, as said below
- tile_cols: int32 [16, 512], P('row', 'col'), may hold values from 0 to 31
- counts: int32 [16, 16], P('row', 'col'), may hold values from 1 to 31, as said below
Outputs:
- basis: float32 [32, 131072], P(None, ('row', 'col'))
- projected: float32 [32, 32], replicated
Inputs may be any that keep to these rules, and one draw needn't show every extreme that they name: `tile_rows`: the 32 (row, column) pairs of one device are distinct. counts[r, c] + counts[r', c] <= 32 where r' differs from r by 8; equality holds in column 0.
All inputs are finite; a program needn't handle non-finite values.
Results may differ from a plain program's by a relative error of at most 0.0003.
Values sent between devices are 32-bit elements; how exact they have to be, the bound alone decides.
A program may use at most 64 MiB of HBM per device.

v0:
```python
import jax
import jax.numpy as jnp
from jax import lax
from jax.sharding import PartitionSpec as P

DEGREE = 3
center_shift = 1.0
spread_radius = 1.4
group_width = 8


def tile_products(blocks, tiles, row_local, col_local, live, row_blocks):
    subspace = blocks.shape[0]
    edge = blocks.shape[2]
    block_ids = jnp.arange(row_blocks, dtype=jnp.int32)

    def add_group(index, total):
        start = index * group_width
        group_tiles = lax.dynamic_slice_in_dim(tiles, start, group_width, 0)
        group_rows = lax.dynamic_slice_in_dim(row_local, start, group_width, 0)
        group_cols = lax.dynamic_slice_in_dim(col_local, start, group_width, 0)
        picked = jnp.take(blocks, group_cols, axis=1)
        product = jnp.einsum("kgj,gij->kgi", picked, group_tiles, precision=lax.Precision.HIGHEST)
        valid = start + jnp.arange(group_width, dtype=jnp.int32) < live
        select = ((group_rows[None, :] == block_ids[:, None]) & valid[None, :]).astype(jnp.float32)
        return total + jnp.einsum("ig,kgb->kib", select, product, precision=lax.Precision.HIGHEST)

    initial = jnp.zeros((subspace, row_blocks, edge), jnp.float32)
    return lax.fori_loop(0, (live + group_width - 1) // group_width, add_group, initial)


def inner_products(left, right):
    return jnp.einsum("kn,mn->km", left, right, precision=lax.Precision.HIGHEST)


def body(start_basis, degrees, tiles, tile_rows, tile_cols, counts):
    subspace = start_basis.shape[0]
    edge = tiles.shape[1]
    row_local = tile_rows[0]
    col_local = tile_cols[0]
    live_count = counts[0, 0]
    row_blocks = lax.axis_size("col") * start_basis.shape[1] // edge
    nverts = lax.axis_size("row") * lax.axis_size("col") * start_basis.shape[1]

    def apply_operator(vectors):
        gathered = lax.all_gather(vectors, "row", axis=1, tiled=True)
        blocks = gathered.reshape(subspace, -1, edge)
        partial_value = tile_products(blocks, tiles, row_local, col_local, live_count, row_blocks)
        summed = lax.psum_scatter(
            partial_value.reshape(subspace, -1), "col", scatter_dimension=1, tiled=True
        )
        return degrees[None, :] * vectors - summed

    def shifted(vectors):
        return (apply_operator(vectors) - center_shift * vectors) / spread_radius

    previous = start_basis
    filtered = shifted(start_basis)
    for level in range(DEGREE - 1):
        following = 2.0 * shifted(filtered) - previous
        previous, filtered = (filtered, following)
    gram_matrix = lax.psum(inner_products(filtered, filtered), ("row", "col")) / nverts
    factor = jnp.linalg.cholesky(gram_matrix)
    basis = jax.scipy.linalg.solve_triangular(factor, filtered, lower=True)
    image = apply_operator(basis)
    moment = lax.psum(inner_products(basis, image), ("row", "col")) / nverts
    projected = 0.5 * (moment + moment.T)
    return (basis, projected)


def solution(mesh):
    return jax.shard_map(
        body,
        mesh=mesh,
        in_specs=(
            P(None, ("row", "col")),
            P(("row", "col")),
            P(("row", "col"), None, None),
            P("row", "col"),
            P("row", "col"),
            P("row", "col"),
        ),
        out_specs=(P(None, ("row", "col")), P()),
        check_vma=False,
    )
```

profile of v0, /device:TPU:1, one launch (start us, length us, event | category | flops | bytes accessed | tf_op | source)
XLA Modules:
  0.0 776.5 jit_solution(2379847340742066916)
XLA Ops:
  8.6 44.0 %all-gather.5.cloned.1.call-done = f32[32,8192]{1,0:T(8,128)} async-done(((f32[32,512]{1,0:T(8,128)}), f32[32,8192]{1,0:T(8,128)}) %all-gather.5.cloned.1.call-update) | async-done | bytes 1048592 | tf_op jit(solution)/shard_map/all_gather | solution.py:46
  54.1 29.0 %while.44 = (s32[]{:T(128)}, f32[32,32,256]{2,1,0:T(8,128)S(1)}, s32[]{:T(128)}, f32[32,256,256]{2,1,0:T(8,128)}, s32[32]{0:T(128)}, /*index=5*/f32[32,32,256]{2...) while((s32[]{:T(128)}, f32[32,32,256]{2,1,0:T(8,128)S(1)}, ...), condition=%wide.region_1.3_spmd.clone, body=%wide.region_0.2_spmd.clone.sunk | while | flops 226821696 | bytes 5509559 | solution.py:29
  56.1 3.6 fusion.122
  63.4 3.6 fusion.122
  70.6 3.6 fusion.122
  77.9 3.6 fusion.122
  84.8 75.6 %reduce-scatter.5.cloned.1.call-done = f32[32,512]{1,0:T(8,128)} async-done(((f32[32,8192]{1,0:T(8,128)}), f32[32,512]{1,0:T(8,128)}) %reduce-scatter.5.cloned.1.call-update) | async-done | bytes 65552 | tf_op jit(solution)/shard_map/reduce_scatter | solution.py:49
  161.9 41.0 %all-gather.7.cloned.1.call-done = f32[32,8192]{1,0:T(8,128)} async-done(((f32[32,512]{1,0:T(8,128)}), f32[32,8192]{1,0:T(8,128)}) %all-gather.7.cloned.1.call-update) | async-done | bytes 1048592 | tf_op jit(solution)/shard_map/all_gather | solution.py:46
  204.4 29.0 %while.45 = (s32[]{:T(128)}, f32[32,32,256]{2,1,0:T(8,128)S(1)}, s32[]{:T(128)}, f32[32,256,256]{2,1,0:T(8,128)}, s32[32]{0:T(128)}, /*index=5*/f32[32,32,256]{2...) while((s32[]{:T(128)}, f32[32,32,256]{2,1,0:T(8,128)S(1)}, ...), condition=%wide.region_4.6_spmd.clone, body=%wide.region_3.5_spmd.clone.sunk | while | flops 226821696 | bytes 5509559 | solution.py:29
  206.4 3.6 fusion.128
  213.6 3.6 fusion.128
  220.9 3.6 fusion.128
  228.1 3.6 fusion.128
  235.1 75.6 %reduce-scatter.7.cloned.1.call-done = f32[32,512]{1,0:T(8,128)} async-done(((f32[32,8192]{1,0:T(8,128)}), f32[32,512]{1,0:T(8,128)}) %reduce-scatter.7.cloned.1.call-update) | async-done | bytes 65552 | tf_op jit(solution)/shard_map/reduce_scatter | solution.py:49
  312.3 40.8 %all-gather.9.cloned.1.call-done = f32[32,8192]{1,0:T(8,128)} async-done(((f32[32,512]{1,0:T(8,128)}), f32[32,8192]{1,0:T(8,128)}) %all-gather.9.cloned.1.call-update) | async-done | bytes 1048592 | tf_op jit(solution)/shard_map/all_gather | solution.py:46
  354.6 29.0 %while.46 = (s32[]{:T(128)}, f32[32,32,256]{2,1,0:T(8,128)S(1)}, s32[]{:T(128)}, f32[32,256,256]{2,1,0:T(8,128)}, s32[32]{0:T(128)}, /*index=5*/f32[32,32,256]{2...) while((s32[]{:T(128)}, f32[32,32,256]{2,1,0:T(8,128)S(1)}, ...), condition=%wide.region_7.9_spmd.clone, body=%wide.region_6.8_spmd.clone.sunk | while | flops 226821696 | bytes 5509559 | solution.py:29
  385.3 75.6 %reduce-scatter.9.cloned.1.call-done = f32[32,512]{1,0:T(8,128)} async-done(((f32[32,8192]{1,0:T(8,128)}), f32[32,512]{1,0:T(8,128)}) %reduce-scatter.9.cloned.1.call-update) | async-done | bytes 65552 | tf_op jit(solution)/shard_map/reduce_scatter | solution.py:49
  462.0 77.5 %psum.14 = f32[32,32]{0,1:T(8,128)S(1)} all-reduce(f32[32,32]{0,1:T(8,128)S(1)} %fusion.89), channel_id=1, replica_groups=mesh['row'=16,'col'=16] {'row','col'}, use_global_device_ids=true, to_apply=%region_9.11 | all-reduce | flops 1024 | bytes 8192 | tf_op jit(solution)/shard_map/psum | solution.py:62
  547.3 35.6 %all-gather.11.cloned.1.call-done = f32[32,8192]{1,0:T(8,128)} async-done(((f32[32,512]{1,0:T(8,128)}), f32[32,8192]{1,0:T(8,128)}) %all-gather.11.cloned.1.call-update) | async-done | bytes 1048592 | tf_op jit(solution)/shard_map/all_gather | solution.py:46
  584.4 29.0 %while.47 = (s32[]{:T(128)}, f32[32,32,256]{2,1,0:T(8,128)S(1)}, s32[]{:T(128)}, f32[32,256,256]{2,1,0:T(8,128)}, s32[32]{0:T(128)}, /*index=5*/f32[32,32,256]{2...) while((s32[]{:T(128)}, f32[32,32,256]{2,1,0:T(8,128)S(1)}, ...), condition=%wide.region_13.15_spmd.clone, body=%wide.region_12.14_spmd.clone.sunk | while | flops 226821696 | bytes 5509559 | solution.py:29
  586.4 3.6 fusion.140
  593.6 3.6 fusion.140
  615.0 75.7 %reduce-scatter.11.cloned.1.call-done = f32[32,512]{1,0:T(8,128)} async-done(((f32[32,8192]{1,0:T(8,128)}), f32[32,512]{1,0:T(8,128)}) %reduce-scatter.11.cloned.1.call-update) | async-done | bytes 65552 | tf_op jit(solution)/shard_map/reduce_scatter | solution.py:49
  691.7 77.3 %psum.15 = f32[32,32]{0,1:T(8,128)S(1)} all-reduce(f32[32,32]{0,1:T(8,128)S(1)} %fusion.80), channel_id=1, replica_groups=mesh['row'=16,'col'=16] {'row','col'}, use_global_device_ids=true, to_apply=%region_15.17 | all-reduce | flops 1024 | bytes 8192 | tf_op jit(solution)/shard_map/psum | solution.py:66
  (144 shorter events, 105.8 us)
Async XLA Ops:
  7.2 45.4 %all-gather.5.cloned.1.call-start = ((), (), s32[]{:S(2)}) async-start(), calls=%async_computation.4 | async-start | bytes 1114112 | tf_op jit(solution)/shard_map/all_gather | solution.py:46
  7.9 152.5 %reduce-scatter.5.cloned.1.call-start = ((), (), s32[]{:S(2)}) async-start(), calls=%async_computation.5 | async-start | bytes 1114112 | tf_op jit(solution)/shard_map/reduce_scatter | solution.py:49
  54.1 106.3 %copy-start = (f32[32,512]{1,0:T(8,128)S(1)}, f32[32,512]{1,0:T(8,128)}, u32[]{:S(2)}) copy-start(f32[32,512]{1,0:T(8,128)} %param.16) | copy-start | bytes 196612
  54.1 106.3 %copy-start.4 = (f32[512]{0:T(512)S(1)}, f32[512]{0:T(512)}, u32[]{:S(2)}) copy-start(f32[512]{0:T(512)} %param.17) | copy-start | bytes 6148
  84.7 118.2 %all-gather.7.cloned.1.call-start = ((), (), s32[]{:S(2)}) async-start(), calls=%async_computation.6 | async-start | bytes 1114112 | tf_op jit(solution)/shard_map/all_gather | solution.py:46
  161.9 148.8 %reduce-scatter.7.cloned.1.call-start = ((), (), s32[]{:S(2)}) async-start(), calls=%async_computation.7 | async-start | bytes 1114112 | tf_op jit(solution)/shard_map/reduce_scatter | solution.py:49
  204.4 106.3 %copy-start.2 = (f32[32,512]{1,0:T(8,128)S(1)}, f32[32,512]{1,0:T(8,128)}, u32[]{:S(2)}) copy-start(f32[32,512]{1,0:T(8,128)} %reduce-scatter.5.cloned.1.call-done) | copy-start | bytes 196612
  235.0 118.1 %all-gather.9.cloned.1.call-start = ((), (), s32[]{:S(2)}) async-start(), calls=%async_computation.8 | async-start | bytes 1114112 | tf_op jit(solution)/shard_map/all_gather | solution.py:46
  312.2 148.7 %reduce-scatter.9.cloned.1.call-start = ((), (), s32[]{:S(2)}) async-start(), calls=%async_computation.9 | async-start | bytes 1114112 | tf_op jit(solution)/shard_map/reduce_scatter | solution.py:49
  354.6 106.3 %copy-start.3 = (f32[32,512]{1,0:T(8,128)S(1)}, f32[32,512]{1,0:T(8,128)}, u32[]{:S(2)}) copy-start(f32[32,512]{1,0:T(8,128)} %multiply_subtract_fusion.1) | copy-start | bytes 196612
  385.2 197.7 %all-gather.11.cloned.1.call-start = ((), (), s32[]{:S(2)}) async-start(), calls=%async_computation.10 | async-start | bytes 1114112 | tf_op jit(solution)/shard_map/all_gather | solution.py:46
  547.2 143.5 %reduce-scatter.11.cloned.1.call-start = ((), (), s32[]{:S(2)}) async-start(), calls=%async_computation.11 | async-start | bytes 1114112 | tf_op jit(solution)/shard_map/reduce_scatter | solution.py:49
  584.4 106.3 %copy-start.1 = (f32[32,512]{1,0:T(8,128)S(1)}, f32[32,512]{1,0:T(8,128)}, u32[]{:S(2)}) copy-start(f32[32,512]{1,0:T(8,128)} %fusion.87) | copy-start | bytes 196612
Sparse Core Ops, SparseCore 0:
  9.8 42.7 all-gather.4
  84.9 75.4 reduce-scatter.4
  162.8 40.0 all-gather.6
  235.1 75.5 reduce-scatter.6
  313.0 40.0 all-gather.8
  385.3 75.5 reduce-scatter.8
  547.4 35.5 all-gather.10
  615.1 75.4 reduce-scatter.10
where the time goes:
time: 778 us; the launch traced here: 777 us
  waiting for transfers between devices  465 us (60%)
  blocking collectives  155 us (20%)
  matrix products  74.3 us (10%)
  other arithmetic  33.4 us (4%)
  local copies, waits for them, and re-layouts  33.2 us (4%)
  between operations  15 us (2%)
    reduce_scatter x4, waiting for transfers between devices, apply_operator(): lax.psum_scatter(partial_value.reshape(subspace, -1), 'col', scatter_dime...  303 us
    all_gather x4, waiting for transfers between devices, apply_operator(): gathered = lax.all_gather(vectors, 'row', axis=1, tiled=True)  161 us
    psum x1, blocking collectives, body(): lax.psum(inner_products(filtered, filtered), ('row', 'col')) / nverts  77.5 us
    psum x1, blocking collectives, body(): moment = lax.psum(inner_products(basis, image), ('row', 'col')) / nverts  77.3 us
    dot_general x16, matrix products, add_group(): jnp.einsum('kgj,gij->kgi', picked, group_tiles, precision=lax.Precision.H...  58.1 us
    and x16, other arithmetic, add_group(): picked = jnp.take(blocks, group_cols, axis=1)  22.1 us
  transfers between devices with their start and end apart: 8, of which 8 were waited for; matrix products, arithmetic and copies ran while one was open for 0% of the time, Pallas kernels for 0%

commit v1 on v0

--- a/solution.py
+++ b/solution.py
@@ -43,7 +43,10 @@
     nverts = lax.axis_size("row") * lax.axis_size("col") * start_basis.shape[1]
 
     def apply_operator(vectors):
-        gathered = lax.all_gather(vectors, "row", axis=1, tiled=True)
+        devices = lax.axis_size("row")
+        shards = jnp.stack([vectors for _ in range(devices)])
+        shards = lax.all_to_all(shards, "row", split_axis=0, concat_axis=0)
+        gathered = jnp.concatenate(shards, axis=1)
         blocks = gathered.reshape(subspace, -1, edge)
         partial_value = tile_products(blocks, tiles, row_local, col_local, live_count, row_blocks)
         summed = lax.psum_scatter(

time: 778 us -> 733 us (0.942)
  waiting for transfers between devices: 465 us -> 402 us
  starting transfers between devices: 0.32 us -> 35.6 us
  other arithmetic: 33.4 us -> 21.7 us
    all_gather x4 -> x0, waiting for transfers between devices: 161 us -> none  [apply_operator(): gathered = lax.all_gather(vectors, 'row', axis=1, tiled=True)]
    all_to_all x0 -> x4, waiting for transfers between devices: none -> 111 us  [apply_operator(): shards = lax.all_to_all(shards, 'row', split_axis=0, concat_axis=0)]
    all_to_all x0 -> x4, starting transfers between devices: none -> 35.3 us  [apply_operator(): shards = lax.all_to_all(shards, 'row', split_axis=0, concat_axis=0)]
    reduce_scatter x4, waiting for transfers between devices: 303 us -> 291 us  [apply_operator(): lax.psum_scatter(partial_value.reshape(subspace, -1), 'col', scatter_dime...]
    and x16, other arithmetic: 22.1 us -> 11.6 us  [add_group(): picked = jnp.take(blocks, group_cols, axis=1)]
    dynamic_slice x16, local copies, waits for them, and re-layouts: 11.7 us -> 1.26 us  [add_group(): group_rows = lax.dynamic_slice_in_dim(row_local, start, group_width, 0)]
where the time goes in v1:
time: 733 us; the launch traced here: 731 us
  waiting for transfers between devices  402 us (55%)
  blocking collectives  155 us (21%)
  matrix products  73.7 us (10%)
  starting transfers between devices  35.6 us (5%)
  local copies, waits for them, and re-layouts  28.1 us (4%)
  other arithmetic  21.7 us (3%)
  between operations  14.7 us (2%)
    reduce_scatter x4, waiting for transfers between devices, apply_operator(): lax.psum_scatter(partial_value.reshape(subspace, -1), 'col', scatter_dime...  291 us
    all_to_all x4, waiting for transfers between devices, apply_operator(): shards = lax.all_to_all(shards, 'row', split_axis=0, concat_axis=0)  111 us
    psum x1, blocking collectives, body(): moment = lax.psum(inner_products(basis, image), ('row', 'col')) / nverts  77.3 us
    psum x1, blocking collectives, body(): lax.psum(inner_products(filtered, filtered), ('row', 'col')) / nverts  77.3 us
    dot_general x16, matrix products, add_group(): jnp.einsum('kgj,gij->kgi', picked, group_tiles, precision=lax.Precision.H...  58.1 us
    all_to_all x4, starting transfers between devices, apply_operator(): shards = lax.all_to_all(shards, 'row', split_axis=0, concat_axis=0)  35.3 us
  transfers between devices with their start and end apart: 8, of which 8 were waited for; matrix products, arithmetic and copies ran while one was open for 0% of the time, Pallas kernels for 0%

profile of v1, /device:TPU:1, one launch (start us, length us, event | category | flops | bytes accessed | tf_op | source)
XLA Modules:
  0.0 731.2 jit_solution(10093240371446845267)
XLA Ops:
  9.1 10.0 %all-to-all-start = ((f32[16,32,512]{2,1,0:T(8,128)}), f32[16,32,512]{2,1,0:T(8,128)S(1)}, u32[]{:S(2)}, u32[]{:S(2)}) async-start(f32[16,32,512]{2,1,0:T(8,128)} %stack.8), calls=%async_computation | async-start | bytes 2097152 | tf_op jit(solution)/shard_map/all_to_all | solution.py:48
  19.8 27.3 %all-to-all-done = f32[16,32,512]{2,1,0:T(8,128)S(1)} async-done(((f32[16,32,512]{2,1,0:T(8,128)}), f32[16,32,512]{2,1,0:T(8,128)S(1)}, u32[]{:S(2)}, u32[]{:S(2)}) %all-to-all-start) | async-done | bytes 1048608 | tf_op jit(solution)/shard_map/all_to_all | solution.py:48
  48.7 23.8 %while.44 = (s32[]{:T(128)}, f32[32,32,256]{2,1,0:T(8,128)S(1)}, s32[]{:T(128)}, f32[32,256,256]{2,1,0:T(8,128)}, s32[32]{0:T(128)S(1)}, /*index=5*/f32[32,32,25...) while((s32[]{:T(128)}, f32[32,32,256]{2,1,0:T(8,128)S(1)}, ...), condition=%wide.region_1.3_spmd.clone, body=%wide.region_0.2_spmd.clone.sunk | while | flops 226821696 | bytes 5509559 | solution.py:29
  50.0 3.6 fusion.122
  55.9 3.6 fusion.122
  74.1 74.8 %reduce-scatter.5.cloned.1.call-done = f32[32,512]{1,0:T(8,128)} async-done(((f32[32,8192]{1,0:T(8,128)}), f32[32,512]{1,0:T(8,128)}) %reduce-scatter.5.cloned.1.call-update) | async-done | bytes 65552 | tf_op jit(solution)/shard_map/reduce_scatter | solution.py:52
  150.8 9.4 %all-to-all-start.1 = ((f32[16,32,512]{2,1,0:T(8,128)}), f32[16,32,512]{2,1,0:T(8,128)S(1)}, u32[]{:S(2)}, u32[]{:S(2)}) async-start(f32[16,32,512]{2,1,0:T(8,128)} %stack.9), calls=%async_computation.2 | async-start | bytes 2097152 | tf_op jit(solution)/shard_map/all_to_all | solution.py:48
  160.2 27.9 %all-to-all-done.1 = f32[16,32,512]{2,1,0:T(8,128)S(1)} async-done(((f32[16,32,512]{2,1,0:T(8,128)}), f32[16,32,512]{2,1,0:T(8,128)S(1)}, u32[]{:S(2)}, u32[]{:S(2)}) %all-to-all-start.1) | async-done | bytes 1048608 | tf_op jit(solution)/shard_map/all_to_all | solution.py:48
  189.7 23.8 %while.45 = (s32[]{:T(128)}, f32[32,32,256]{2,1,0:T(8,128)S(1)}, s32[]{:T(128)}, f32[32,256,256]{2,1,0:T(8,128)}, s32[32]{0:T(128)S(1)}, /*index=5*/f32[32,32,25...) while((s32[]{:T(128)}, f32[32,32,256]{2,1,0:T(8,128)S(1)}, ...), condition=%wide.region_4.6_spmd.clone, body=%wide.region_3.5_spmd.clone.sunk | while | flops 226821696 | bytes 5509559 | solution.py:29
  191.0 3.6 fusion.128
  208.8 3.6 fusion.128
  215.1 72.7 %reduce-scatter.7.cloned.1.call-done = f32[32,512]{1,0:T(8,128)} async-done(((f32[32,8192]{1,0:T(8,128)}), f32[32,512]{1,0:T(8,128)}) %reduce-scatter.7.cloned.1.call-update) | async-done | bytes 65552 | tf_op jit(solution)/shard_map/reduce_scatter | solution.py:52
  289.8 9.3 %all-to-all-start.2 = ((f32[16,32,512]{2,1,0:T(8,128)}), f32[16,32,512]{2,1,0:T(8,128)S(1)}, u32[]{:S(2)}, u32[]{:S(2)}) async-start(f32[16,32,512]{2,1,0:T(8,128)} %stack.10), calls=%async_computation.4 | async-start | bytes 2097152 | tf_op jit(solution)/shard_map/all_to_all | solution.py:48
  299.3 27.8 %all-to-all-done.2 = f32[16,32,512]{2,1,0:T(8,128)S(1)} async-done(((f32[16,32,512]{2,1,0:T(8,128)}), f32[16,32,512]{2,1,0:T(8,128)S(1)}, u32[]{:S(2)}, u32[]{:S(2)}) %all-to-all-start.2) | async-done | bytes 1048608 | tf_op jit(solution)/shard_map/all_to_all | solution.py:48
  328.6 23.8 %while.46 = (s32[]{:T(128)}, f32[32,32,256]{2,1,0:T(8,128)S(1)}, s32[]{:T(128)}, f32[32,256,256]{2,1,0:T(8,128)}, s32[32]{0:T(128)S(1)}, /*index=5*/f32[32,32,25...) while((s32[]{:T(128)}, f32[32,32,256]{2,1,0:T(8,128)S(1)}, ...), condition=%wide.region_7.9_spmd.clone, body=%wide.region_6.8_spmd.clone.sunk | while | flops 226821696 | bytes 5509559 | solution.py:29
  354.0 72.7 %reduce-scatter.9.cloned.1.call-done = f32[32,512]{1,0:T(8,128)} async-done(((f32[32,8192]{1,0:T(8,128)}), f32[32,512]{1,0:T(8,128)}) %reduce-scatter.9.cloned.1.call-update) | async-done | bytes 65552 | tf_op jit(solution)/shard_map/reduce_scatter | solution.py:52
  427.8 77.3 %psum.14 = f32[32,32]{0,1:T(8,128)S(1)} all-reduce(f32[32,32]{0,1:T(8,128)S(1)} %fusion.89), channel_id=1, replica_groups=mesh['row'=16,'col'=16] {'row','col'}, use_global_device_ids=true, to_apply=%region_9.11 | all-reduce | flops 1024 | bytes 8192 | tf_op jit(solution)/shard_map/psum | solution.py:65
  513.3 6.6 all-to-all-start.3
  520.0 27.9 %all-to-all-done.3 = f32[16,32,512]{2,1,0:T(8,128)S(1)} async-done(((f32[16,32,512]{2,1,0:T(8,128)}), f32[16,32,512]{2,1,0:T(8,128)S(1)}, u32[]{:S(2)}, u32[]{:S(2)}) %all-to-all-start.3) | async-done | bytes 1048608 | tf_op jit(solution)/shard_map/all_to_all | solution.py:48
  549.4 23.8 %while.47 = (s32[]{:T(128)}, f32[32,32,256]{2,1,0:T(8,128)S(1)}, s32[]{:T(128)}, f32[32,256,256]{2,1,0:T(8,128)}, s32[32]{0:T(128)S(1)}, /*index=5*/f32[32,32,25...) while((s32[]{:T(128)}, f32[32,32,256]{2,1,0:T(8,128)S(1)}, ...), condition=%wide.region_13.15_spmd.clone, body=%wide.region_12.14_spmd.clone.sunk | while | flops 226821696 | bytes 5509559 | solution.py:29
  550.8 3.6 fusion.140
  556.7 3.6 fusion.140
  574.8 70.8 %reduce-scatter.11.cloned.1.call-done = f32[32,512]{1,0:T(8,128)} async-done(((f32[32,8192]{1,0:T(8,128)}), f32[32,512]{1,0:T(8,128)}) %reduce-scatter.11.cloned.1.call-update) | async-done | bytes 65552 | tf_op jit(solution)/shard_map/reduce_scatter | solution.py:52
  646.7 77.3 %psum.15 = f32[32,32]{0,1:T(8,128)S(1)} all-reduce(f32[32,32]{0,1:T(8,128)S(1)} %fusion.80), channel_id=1, replica_groups=mesh['row'=16,'col'=16] {'row','col'}, use_global_device_ids=true, to_apply=%region_15.17 | all-reduce | flops 1024 | bytes 8192 | tf_op jit(solution)/shard_map/psum | solution.py:69
  (154 shorter events, 102.2 us)
Async XLA Ops:
  7.2 41.5 %copy-start.3 = (s32[1,32]{1,0:T(1,128)S(1)}, s32[1,32]{1,0:T(1,128)}, u32[]{:S(2)}) copy-start(s32[1,32]{1,0:T(1,128)} %param.20) | copy-start | bytes 388
  7.2 41.5 %copy-start.5 = (s32[1,32]{1,0:T(1,128)S(1)}, s32[1,32]{1,0:T(1,128)}, u32[]{:S(2)}) copy-start(s32[1,32]{1,0:T(1,128)} %param.19) | copy-start | bytes 388
  9.1 38.0 %all-to-all-start = ((f32[16,32,512]{2,1,0:T(8,128)}), f32[16,32,512]{2,1,0:T(8,128)S(1)}, u32[]{:S(2)}, u32[]{:S(2)}) async-start(f32[16,32,512]{2,1,0:T(8,128)} %stack.8), calls=%async_computation | async-start | bytes 2097152 | tf_op jit(solution)/shard_map/all_to_all | solution.py:48
  19.1 129.7 %reduce-scatter.5.cloned.1.call-start = ((), (), s32[]{:S(2)}) async-start(), calls=%async_computation.8 | async-start | bytes 1114112 | tf_op jit(solution)/shard_map/reduce_scatter | solution.py:52
  48.6 100.2 %copy-start = (f32[32,512]{1,0:T(8,128)S(1)}, f32[32,512]{1,0:T(8,128)}, u32[]{:S(2)}) copy-start(f32[32,512]{1,0:T(8,128)} %param.16) | copy-start | bytes 196612
  48.6 100.2 %copy-start.4 = (f32[512]{0:T(512)S(1)}, f32[512]{0:T(512)}, u32[]{:S(2)}) copy-start(f32[512]{0:T(512)} %param.17) | copy-start | bytes 6148
  150.8 37.4 %all-to-all-start.1 = ((f32[16,32,512]{2,1,0:T(8,128)}), f32[16,32,512]{2,1,0:T(8,128)S(1)}, u32[]{:S(2)}, u32[]{:S(2)}) async-start(f32[16,32,512]{2,1,0:T(8,128)} %stack.9), calls=%async_computation.2 | async-start | bytes 2097152 | tf_op jit(solution)/shard_map/all_to_all | solution.py:48
  160.2 127.6 %reduce-scatter.7.cloned.1.call-start = ((), (), s32[]{:S(2)}) async-start(), calls=%async_computation.9 | async-start | bytes 1114112 | tf_op jit(solution)/shard_map/reduce_scatter | solution.py:52
  189.7 98.1 %copy-start.2 = (f32[32,512]{1,0:T(8,128)S(1)}, f32[32,512]{1,0:T(8,128)}, u32[]{:S(2)}) copy-start(f32[32,512]{1,0:T(8,128)} %reduce-scatter.5.cloned.1.call-done) | copy-start | bytes 196612
  289.8 37.3 %all-to-all-start.2 = ((f32[16,32,512]{2,1,0:T(8,128)}), f32[16,32,512]{2,1,0:T(8,128)S(1)}, u32[]{:S(2)}, u32[]{:S(2)}) async-start(f32[16,32,512]{2,1,0:T(8,128)} %stack.10), calls=%async_computation.4 | async-start | bytes 2097152 | tf_op jit(solution)/shard_map/all_to_all | solution.py:48
  299.1 127.6 %reduce-scatter.9.cloned.1.call-start = ((), (), s32[]{:S(2)}) async-start(), calls=%async_computation.10 | async-start | bytes 1114112 | tf_op jit(solution)/shard_map/reduce_scatter | solution.py:52
  512.2 133.5 %copy-start.1 = (f32[32,512]{1,0:T(8,128)}, f32[32,512]{1,0:T(8,128)S(1)}, u32[]{:S(2)}) copy-start(f32[32,512]{1,0:T(8,128)S(1)} %fusion.87) | copy-start | bytes 196612
  513.3 34.6 %all-to-all-start.3 = ((f32[16,32,512]{2,1,0:T(8,128)}), f32[16,32,512]{2,1,0:T(8,128)S(1)}, u32[]{:S(2)}, u32[]{:S(2)}) async-start(f32[16,32,512]{2,1,0:T(8,128)} %stack.11), calls=%async_computation.6 | async-start | bytes 2097152 | tf_op jit(solution)/shard_map/all_to_all | solution.py:48
  519.9 125.7 %reduce-scatter.11.cloned.1.call-start = ((), (), s32[]{:S(2)}) async-start(), calls=%async_computation.11 | async-start | bytes 1114112 | tf_op jit(solution)/shard_map/reduce_scatter | solution.py:52
Sparse Core Ops, SparseCore 0:
  74.2 74.5 reduce-scatter.4
  215.2 72.5 reduce-scatter.6
  354.1 72.4 reduce-scatter.8
  574.9 70.6 reduce-scatter.10
